TPU v7x, 32 devices: a whole 2x2x4 slice. The times are simulated.
32 devices in a mesh: comp: 2 (over core), face: 4 (over y, x), tile: 4 (over z).
Axes of the slice: x: 2, y: 2, z: 4, core: 2. Of those that a mesh axis runs over, the one named last changes fastest.
Arguments:
- tokens: bfloat16 [2, 256, 64, 512], P('comp', 'tile', 'face'), may hold values from -6 to 6
- norm_gains: bfloat16 [2, 3, 512], P('comp'), may hold values from 0.5 to 1.5
- qkv_weight: bfloat16 [2, 512, 1536], P('comp'), may hold values from -0.25 to 0.25
- out_weight: bfloat16 [2, 512, 512], P('comp'), may hold values from -0.25 to 0.25
- cross_query: bfloat16 [2, 512, 512], P('comp'), may hold values from -0.25 to 0.25
- cross_kv: bfloat16 [2, 512, 1024], P('comp'), may hold values from -0.25 to 0.25
- cross_out: bfloat16 [2, 512, 512], P('comp'), may hold values from -0.25 to 0.25
- up_weight: bfloat16 [2, 512, 2048], P('comp'), may hold values from -0.25 to 0.25
- down_weight: bfloat16 [2, 2048, 512], P('comp'), may hold values from -0.125 to 0.125
- intersection_list: int32 [2, 32, 4, 4], P(None, 'tile', 'face'), may hold values from 0 to 7, all different within a row
- land_bands: int32 [4, 4], replicated, may hold values from 0 to 7
Outputs:
- evolved: bfloat16 [2, 256, 64, 512], P('comp', 'tile', 'face')
Inputs may be any that keep to these rules, and one draw needn't show every extreme that they name: `intersection_list`: each band names 4 different bands of the other component's tile. `land_bands`: the land bands of an ocean tile are its first ones.
All inputs are finite; a program needn't handle non-finite values.
Results may differ from a plain program's by a relative error of at most 0.0045.
Values may be sent and summed in bfloat16 or wider, within the bound.
A program may use at most 128 MiB of HBM per device.

v0:
```python
import functools

import jax
import jax.numpy as jnp
from jax import lax
from jax.experimental import pallas as pl
from jax.experimental.pallas import tpu as pltpu
from jax.sharding import PartitionSpec as P

HEADS = 8
BR = 8
KC = 4
EPSILON = 1e-05
EXTRA = 16
MESH = pl.DeviceIdType.MESH
F32 = jnp.float32
BF16 = jnp.bfloat16


def dot(a, b):
    return lax.dot_general(a, b, (((1,), (0,)), ((), ())), preferred_element_type=F32)


def dot_t(a, b):
    return lax.dot_general(a, b, (((1,), (1,)), ((), ())), preferred_element_type=F32)


def attend_bands(start, end, pairs, pair, keys_of, values_of, queries, result, scores, terms, peaks):
    cells = queries.shape[2] // 2

    def score(b, p, slot):
        q = queries[b, p]
        top = jnp.zeros((8, 2 * cells), F32)
        row = 0
        for keys in keys_of(b, p):
            rows = keys.shape[0]
            s = dot_t(keys, q)
            scores[slot][pl.ds(row, rows), :] = s
            top = jnp.maximum(top, jnp.max(s.reshape(rows // 8, 8, 2 * cells), axis=0))
            row += rows
        peaks[slot][...] = jnp.broadcast_to(jnp.max(top, axis=0, keepdims=True), (8, 2 * cells))

    def blend(b, p, slot):
        blended = dot(values_of(b, p), terms[slot][...])
        inverse = 1.0 / (blended[pair : pair + 1, :] + peaks[2 + slot][0:1, :])
        first = blended[: pair // 2, :cells] * inverse[:, :cells]
        second = blended[pair // 2 : pair, cells:] * inverse[:, cells:]
        result[b, :, pl.ds(p * pair, pair)] = jnp.concatenate([first, second], axis=0).T.astype(BF16)

    def weigh(slot):
        peak = peaks[slot][0:1, :]
        terms[slot][...] = jnp.exp(scores[slot][...] - peak).astype(BF16)
        peaks[2 + slot][...] = jnp.broadcast_to(jnp.exp(-peak), (8, 2 * cells))

    last = (pairs - 1) % 2
    terms[last][...] = jnp.zeros(terms[last].shape, BF16)
    peaks[2 + last][...] = jnp.ones(peaks[2 + last].shape, F32)
    score(start, 0, 0)

    @pl.loop(start, end)
    def _(b):
        for p in range(pairs):
            slot = p % 2
            if p + 1 < pairs:
                score(b, p + 1, 1 - slot)
            else:
                score(jnp.minimum(b + 1, end - 1), 0, 1 - slot)
            if p > 0:
                blend(b, p - 1, 1 - slot)
            else:
                blend(jnp.maximum(b - 1, start), pairs - 1, 1 - slot)
            weigh(slot)

    blend(end - 1, pairs - 1, last)


def kernel(
    links,
    land,
    tok5,
    tok4,
    gains_hbm,
    wqkv_hbm,
    wout_hbm,
    wcq_hbm,
    wckv_hbm,
    wcout_hbm,
    wup_hbm,
    wdown_hbm,
    out_ref,
    own,
    side,
    ends,
    part,
    gains,
    gains_p,
    wqkv,
    wout,
    wcq,
    wckv,
    wcout,
    wup,
    wdown,
    wv_t,
    qbd,
    cqbd,
    kwin,
    vwin,
    kcross,
    vcross,
    win_res,
    cross_res,
    cs0,
    cs1,
    ce0,
    ce1,
    ws0,
    ws1,
    we0,
    we1,
    m0,
    m1,
    m2,
    m3,
    send_sem,
    recv_sem,
    local_sem,
):
    nb, groups, _, d = own.shape
    cells = groups * BR
    pair = 2 * (d // HEADS)
    pairs = d // pair
    vrows = pair + EXTRA
    comp, face, tile = (lax.axis_index(a) for a in ("comp", "face", "tile"))
    n_face, n_tile = lax.axis_size("face"), lax.axis_size("tile")
    left, right = lax.rem(face + n_face - 1, n_face), lax.rem(face + 1, n_face)
    up, down = lax.rem(tile + n_tile - 1, n_tile), lax.rem(tile + 1, n_tile)
    other = 1 - comp

    local = [
        pltpu.make_async_copy(src, dst, local_sem.at[i])
        for i, (src, dst) in enumerate(
            (
                (tok4, own),
                (gains_hbm, gains),
                (wqkv_hbm, wqkv),
                (wcq_hbm, wcq),
                (wcout_hbm, wcout),
                (wout_hbm, wout),
                (wup_hbm, wup),
                (wdown_hbm, wdown),
            )
        )
    ]
    for copy in local[:4]:
        copy.start()

    barrier = pltpu.get_barrier_semaphore()
    for target in ({"comp": other}, {"face": left}, {"face": right}, {"tile": up}, {"tile": down}):
        pl.semaphore_signal(barrier, inc=1, device_id=target, device_id_type=MESH)
    pl.semaphore_wait(barrier, 5)

    def remote(i, src, dst, target):
        return pltpu.make_async_remote_copy(
            src_ref=src,
            dst_ref=dst,
            send_sem=send_sem.at[i],
            recv_sem=recv_sem.at[i],
            device_id=target,
            device_id_type=MESH,
        )

    def to_face(i, first, count):
        bands = pl.ds(first, count)
        return [
            remote(i, tok5.at[bands, :, 0], side.at[pl.ds(1 + first, count), pl.ds(BR, BR)], {"face": left}),
            remote(i + 1, tok5.at[bands, :, 1], side.at[pl.ds(1 + first, count), pl.ds(0, BR)], {"face": right}),
        ]

    edge_copies = to_face(0, 0, 1) + to_face(2, nb - 1, 1)
    step = nb // 2
    near_copies = to_face(4, 1, step)
    far_copies = to_face(13, 1 + step, nb - 2 - step)
    end_copies = [
        remote(6, tok4.at[0], ends.at[1], {"tile": up}),
        remote(7, tok4.at[nb - 1], ends.at[0], {"tile": down}),
    ]
    comp_copies = [
        remote(8, tok4, part, {"comp": other}),
        remote(9, wckv_hbm, wckv, {"comp": other}),
        remote(10, gains_hbm, gains_p, {"comp": other}),
    ]
    corner_copies = [
        remote(11, side.at[1], side.at[nb + 1], {"tile": up}),
        remote(12, side.at[nb], side.at[0], {"tile": down}),
    ]
    for copy in edge_copies + comp_copies + end_copies + near_copies + far_copies:
        copy.start()
    for copy in local[4:]:
        copy.start()

    is_air = comp == 0
    own_land = land[tile, face]

    def flag(cond):
        return jnp.where(cond, 1.0, 0.0).astype(F32)

    def usable(tile_at, face_at, band):
        return flag(is_air | (band >= land[tile_at, face_at]))

    def scaled(x):
        mean_square = jnp.mean(x * x, axis=-1, keepdims=True)
        return x * lax.rsqrt(mean_square + EPSILON)

    def expand(flags, counts, axis):
        shape = (sum(counts), 1) if axis == 0 else (1, sum(counts))
        at = lax.broadcasted_iota(jnp.int32, shape, axis)
        mask = jnp.full(shape, flags[0], F32)
        start = 0
        for value, count in zip(flags[1:], counts[:-1]):
            start += count
            mask = jnp.where(at >= start, value, mask)
        return mask

    def put_values(ref, at, lanes, vals, mask_row):
        width = vals.shape[1]
        extra = jnp.broadcast_to(mask_row, (EXTRA, width)).astype(BF16)
        for p in range(pairs):
            ref[at, pl.ds(p * vrows, pair), lanes] = vals[p * pair : (p + 1) * pair, :]
            ref[at, pl.ds(p * vrows + pair, EXTRA), lanes] = extra

    def put_queries(ref, b, q):
        lane = lax.broadcasted_iota(jnp.int32, (1, d), 1)
        low = lax.rem(lane, pair) < pair // 2
        q = q * float((d // HEADS) ** -0.5)
        q_low = jnp.where(low, q, 0.0).astype(BF16)
        q_high = jnp.where(low, 0.0, q).astype(BF16)
        for p in range(pairs):
            ref[b, p, pl.ds(0, cells)] = q_low[:, p * pair : (p + 1) * pair]
            ref[b, p, pl.ds(cells, cells)] = q_high[:, p * pair : (p + 1) * pair]

    for copy in local[:4]:
        copy.wait()
    wv_t[0] = wqkv[:, 2 * d : 3 * d].T
    chunk = step * cells

    @pl.loop(0, nb // step)
    def _(c):
        base = c * step
        x = own[pl.ds(base, step)].astype(F32).reshape(chunk, d)
        x = scaled(x)
        flags = [usable(tile, face, base + j) for j in range(step)]
        xa = (x * gains[0:1, :].astype(F32) * expand(flags, [cells] * step, 0)).astype(BF16)
        xc = (x * gains[1:2, :].astype(F32)).astype(BF16)
        q = dot(xa, wqkv[:, 0:d])
        cq = dot(xc, wcq[...])
        k = dot(xa, wqkv[:, d : 2 * d]).astype(BF16)
        v = dot_t(wv_t[0], xa).astype(BF16)
        for j in range(step):
            rows = slice(j * cells, (j + 1) * cells)
            put_queries(qbd, base + j, q[rows])
            put_queries(cqbd, base + j, cq[rows])
            kwin[1 + base + j, pl.ds(0, cells)] = k[rows]
            put_values(vwin, 1 + base + j, pl.ds(0, cells), v[:, rows], jnp.full((1, cells), flags[j], F32))

    for copy in edge_copies:
        copy.wait_recv()
    for copy in corner_copies:
        copy.start()
    for copy in comp_copies:
        copy.wait_recv()
    wv_t[1] = wckv[:, d : 2 * d].T

    @pl.loop(0, nb // step)
    def _(c):
        base = c * step
        x = scaled(part[pl.ds(base, step)].astype(F32).reshape(chunk, d))
        flags = [flag((comp == 1) | (base + j >= own_land)) for j in range(step)]
        xp = (x * gains_p[1:2, :].astype(F32) * expand(flags, [cells] * step, 0)).astype(BF16)
        k = dot(xp, wckv[:, 0:d]).astype(BF16)
        v = dot_t(wv_t[1], xp).astype(BF16)
        for j in range(step):
            rows = slice(j * cells, (j + 1) * cells)
            kcross[base + j] = k[rows]
            put_values(vcross, base + j, pl.ds(0, cells), v[:, rows], jnp.full((1, cells), flags[j], F32))

    def cross_keys(b, p):
        return [kcross[links[comp, b, j], :, pl.ds(p * pair, pair)] for j in range(KC)]

    def cross_values(b, p):
        return jnp.concatenate([vcross[links[comp, b, j], pl.ds(p * vrows, vrows)] for j in range(KC)], axis=1)

    attend_bands(
        0, nb, pairs, pair, cross_keys, cross_values, cqbd, cross_res,
        (cs0, cs1), (ce0, ce1), (m0, m1, m2, m3),
    )

    def window_kv(x, mask_col):
        xa = (scaled(x) * gains[0:1, :].astype(F32) * mask_col).astype(BF16)
        return dot(xa, wqkv[:, d : 2 * d]).astype(BF16), dot_t(wv_t[0], xa).astype(BF16)

    half = cells // 2

    def beside(bands):
        flags = []
        for at in bands:
            flags += [usable(tile, left, at), usable(tile, right, at)]
        x = jnp.concatenate([side[1 + at].astype(F32).reshape(cells, d) for at in bands], axis=0)
        k, v = window_kv(x, expand(flags, [half] * len(flags), 0))
        for j, at in enumerate(bands):
            rows = slice(j * cells, (j + 1) * cells)
            kwin[1 + at, pl.ds(cells, cells)] = k[rows]
            put_values(
                vwin, 1 + at, pl.ds(cells, cells), v[:, rows], expand(flags[2 * j : 2 * j + 2], [half] * 2, 1)
            )

    for copy in end_copies + corner_copies:
        copy.wait_recv()
    above, below = flag(tile > 0), flag(tile < n_tile - 1)
    flags, counts = [], [cells, half, half]
    for inside, row, band in ((above, up, nb - 1), (below, down, 0)):
        flags.append([inside * usable(row, at, band) for at in (face, left, right)])
    rim = jnp.concatenate(
        [ref[at].astype(F32).reshape(cells, d) for ref, at in ((ends, 0), (side, 0), (ends, 1), (side, nb + 1))],
        axis=0,
    )
    k, v = window_kv(rim, expand(flags[0] + flags[1], counts + counts, 0))
    for j, at in enumerate((0, nb + 1)):
        rows = slice(j * 2 * cells, (j + 1) * 2 * cells)
        kwin[at] = k[rows]
        put_values(vwin, at, pl.ds(0, 2 * cells), v[:, rows], expand(flags[j], counts, 1))
    beside((0, nb - 1))

    def window_keys(b, p):
        return [kwin[b + j, :, pl.ds(p * pair, pair)] for j in range(3)]

    def window_values(b, p):
        return jnp.concatenate([vwin[b + j, pl.ds(p * vrows, vrows)] for j in range(3)], axis=1)

    ff = wup.shape[1]
    part_ff = ff // 4

    def finish(base):
        live = expand([flag(is_air | (base + j >= own_land)) for j in range(step)], [cells] * step, 0)
        update = dot(win_res[pl.ds(base, step)].reshape(chunk, d), wout[...])
        update = update + dot(cross_res[pl.ds(base, step)].reshape(chunk, d), wcout[...])
        middle = own[pl.ds(base, step)].astype(F32).reshape(chunk, d) + live * update
        mlp_input = (scaled(middle) * gains[2:3, :].astype(F32)).astype(BF16)
        total = None
        for f in range(4):
            cols = slice(f * part_ff, (f + 1) * part_ff)
            hidden = jax.nn.silu(dot(mlp_input, wup[:, cols])).astype(BF16)
            piece = dot(hidden, wdown[cols, :])
            total = piece if total is None else total + piece
        out_ref[pl.ds(base * cells, chunk), :] = (middle + live * total).astype(BF16)

    for base, copies, bands in (
        (0, near_copies, range(1, 1 + step)),
        (step, far_copies, range(1 + step, nb - 1)),
    ):
        for copy in copies:
            copy.wait_recv()
        beside(bands)
        attend_bands(
            base, base + step, pairs, pair, window_keys, window_values, qbd, win_res,
            (ws0, ws1), (we0, we1), (m0, m1, m2, m3),
        )
        if base == 0:
            for copy in local[4:]:
                copy.wait()
        finish(base)

    for copy in edge_copies + near_copies + far_copies + end_copies + comp_copies + corner_copies:
        copy.wait_send()


def per_device(
    tokens,
    norm_gains,
    qkv_weight,
    out_weight,
    cross_query,
    cross_kv,
    cross_out,
    up_weight,
    down_weight,
    intersection_list,
    land_bands,
):
    _, rows, cols, d = tokens.shape
    nb = rows // BR
    cells = BR * cols
    groups = cells // BR
    ff = up_weight.shape[2]
    pair = 2 * (d // HEADS)
    vrows = (d // pair) * (pair + EXTRA)
    links = intersection_list.reshape(2, nb, KC)
    smem = pl.BlockSpec(memory_space=pltpu.SMEM)
    hbm = pl.BlockSpec(memory_space=pl.ANY)
    out = pl.pallas_call(
        kernel,
        out_shape=jax.ShapeDtypeStruct((nb * cells, d), BF16),
        in_specs=[smem] * 2 + [hbm] * 10,
        out_specs=pl.BlockSpec(memory_space=pltpu.VMEM),
        scratch_shapes=[
            pltpu.VMEM((nb, groups, BR, d), BF16),
            pltpu.VMEM((nb + 2, groups, BR, d), BF16),
            pltpu.VMEM((2, groups, BR, d), BF16),
            pltpu.VMEM((nb, groups, BR, d), BF16),
            pltpu.VMEM((3, d), BF16),
            pltpu.VMEM((3, d), BF16),
            pltpu.VMEM((d, 3 * d), BF16),
            pltpu.VMEM((d, d), BF16),
            pltpu.VMEM((d, d), BF16),
            pltpu.VMEM((d, 2 * d), BF16),
            pltpu.VMEM((d, d), BF16),
            pltpu.VMEM((d, ff), BF16),
            pltpu.VMEM((ff, d), BF16),
            pltpu.VMEM((2, d, d), BF16),
            pltpu.VMEM((nb, d // pair, 2 * cells, pair), BF16),
            pltpu.VMEM((nb, d // pair, 2 * cells, pair), BF16),
            pltpu.VMEM((nb + 2, 2 * cells, d), BF16),
            pltpu.VMEM((nb + 2, vrows, 2 * cells), BF16),
            pltpu.VMEM((nb, cells, d), BF16),
            pltpu.VMEM((nb, vrows, cells), BF16),
            pltpu.VMEM((nb, cells, d), BF16),
            pltpu.VMEM((nb, cells, d), BF16),
            *[pltpu.VMEM((KC * cells, 2 * cells), F32)] * 2,
            *[pltpu.VMEM((KC * cells, 2 * cells), BF16)] * 2,
            *[pltpu.VMEM((6 * cells, 2 * cells), F32)] * 2,
            *[pltpu.VMEM((6 * cells, 2 * cells), BF16)] * 2,
            *[pltpu.VMEM((8, 2 * cells), F32)] * 4,
            pltpu.SemaphoreType.DMA((15,)),
            pltpu.SemaphoreType.DMA((15,)),
            pltpu.SemaphoreType.DMA((8,)),
        ],
        compiler_params=pltpu.CompilerParams(
            collective_id=0, has_side_effects=True, vmem_limit_bytes=56 * 1024 * 1024
        ),
    )(
        links,
        land_bands,
        tokens.reshape(nb, BR, cols // BR, BR, d),
        tokens.reshape(nb, groups, BR, d),
        norm_gains[0],
        qkv_weight[0],
        out_weight[0],
        cross_query[0],
        cross_kv[0],
        cross_out[0],
        up_weight[0],
        down_weight[0],
    )
    return out.reshape(1, rows, cols, d)


def solution(mesh):
    placed = (
        P("comp", "tile", "face", None),
        P("comp", None, None),
        P("comp", None, None),
        P("comp", None, None),
        P("comp", None, None),
        P("comp", None, None),
        P("comp", None, None),
        P("comp", None, None),
        P("comp", None, None),
        P(None, "tile", "face", None),
        P(),
    )
    return jax.shard_map(
        per_device,
        mesh=mesh,
        in_specs=placed,
        out_specs=P("comp", "tile", "face", None),
        check_vma=False,
    )
```

profile of v0, /device:TPU:0, one launch (start us, length us, event | category | flops | bytes accessed | tf_op | source)
XLA Modules:
  0.0 49.7 jit_solution(12932522632675373471)
XLA Ops:
  0.0 1.4 %copy.12.links = s32[2,8,4]{2,1,0:T(8,128)} copy(s32[2,8,4]{1,2,0:T(4,128)} %bitcast.23) | data formatting | bytes 512 | tf_op jit(solution)/shard_map/reshape | solution.py:397
  1.4 46.0 %shard_map.109 = bf16[1024,512]{1,0:T(8,128)(2,1)} custom-call(s32[2,8,4]{2,1,0:T(8,128)} %copy.12.links, s32[4,4]{1,0:T(4,128)} %land.1, bf16[8,8,2,8,512]{4,3,2,1,0:T(8,128)(2,1)} %bitcast.12, bf16[8,16,8,512]{3,2,1,0:T(8,128)(2,1)} %bitcast.13, bf16[3,512]{1,0:T(4,128)(2,1)} %bitcast.22, bf16[512,1536]{1,0:T(8,128)(2,1)} %bitcast.17, ...), custom_call_target="tpu_custom_call" | custom-call | tf_op jit(solution)/shard_map/pallas_call | solution.py:400
  47.4 2.3 %copy.14 = bf16[1,64,16,512]{3,2,1,0:T(8,128)(2,1)} copy(bf16[1,64,16,512]{3,2,1,0:T(8,128)(2,1)} %bitcast.14) | data formatting | bytes 2097152
where the time goes:
time: 50 us; the launch traced here: 49.7 us
  Pallas kernels  46 us (92%)
  local copies, waits for them, and re-layouts  3.63 us (7%)
    pallas_call x1, Pallas kernels, per_device(): pl.pallas_call(kernel, out_shape=jax.ShapeDtypeStruct((nb * cells, d), BF...  46 us
    unnamed x1, local copies, waits for them, and re-layouts  2.26 us
    reshape x1, local copies, waits for them, and re-layouts, per_device(): links = intersection_list.reshape(2, nb, KC)  1.36 us

commit v1 on v0

--- a/solution.py
+++ b/solution.py
@@ -12,6 +12,7 @@
 KC = 4
 EPSILON = 1e-05
 EXTRA = 16
+LOG2E = 1.4426950408889634
 MESH = pl.DeviceIdType.MESH
 F32 = jnp.float32
 BF16 = jnp.bfloat16
@@ -25,12 +26,15 @@
     return lax.dot_general(a, b, (((1,), (1,)), ((), ())), preferred_element_type=F32)
 
 
-def attend_bands(start, end, pairs, pair, keys_of, values_of, queries, result, scores, terms, peaks):
+def attend_bands(start, end, pairs, pair, keys_of, values_of, queries, scores, terms, peaks, result=None, held=None):
     cells = queries.shape[2] // 2
+    half = pair // 2
 
     def score(b, p, slot):
         q = queries[b, p]
         top = jnp.zeros((8, 2 * cells), F32)
+        if result is not None and held is not None:
+            top = held[2][b, p]
         row = 0
         for keys in keys_of(b, p):
             rows = keys.shape[0]
@@ -42,19 +46,38 @@
 
     def blend(b, p, slot):
         blended = dot(values_of(b, p), terms[slot][...])
-        inverse = 1.0 / (blended[pair : pair + 1, :] + peaks[2 + slot][0:1, :])
-        first = blended[: pair // 2, :cells] * inverse[:, :cells]
-        second = blended[pair // 2 : pair, cells:] * inverse[:, cells:]
+        first, second = blended[:half, :cells], blended[half:pair, cells:]
+        total = blended[pair : pair + 8, :]
+        if result is None:
+            held[0][b, p, :, pl.ds(0, cells)] = first
+            held[0][b, p, :, pl.ds(cells, cells)] = second
+            held[1][b, p] = total
+            return
+        total = total[0:1, :] + peaks[2 + slot][0:1, :]
+        if held is not None:
+            fade = peaks[4 + slot][0:1, :]
+            total = total + held[1][b, p, 0:1, :] * fade
+            first = first + held[0][b, p, :, pl.ds(0, cells)] * fade[:, :cells]
+            second = second + held[0][b, p, :, pl.ds(cells, cells)] * fade[:, cells:]
+        inverse = 1.0 / total
+        first = first * inverse[:, :cells]
+        second = second * inverse[:, cells:]
         result[b, :, pl.ds(p * pair, pair)] = jnp.concatenate([first, second], axis=0).T.astype(BF16)
 
-    def weigh(slot):
+    def weigh(b, p, slot):
         peak = peaks[slot][0:1, :]
-        terms[slot][...] = jnp.exp(scores[slot][...] - peak).astype(BF16)
-        peaks[2 + slot][...] = jnp.broadcast_to(jnp.exp(-peak), (8, 2 * cells))
+        terms[slot][...] = jnp.exp2(scores[slot][...] - peak).astype(BF16)
+        if result is None:
+            held[2][b, p] = peaks[slot][...]
+            return
+        peaks[2 + slot][...] = jnp.exp2(-peaks[slot][...])
+        if held is not None:
+            peaks[4 + slot][...] = jnp.exp2(held[2][b, p] - peaks[slot][...])
 
     last = (pairs - 1) % 2
     terms[last][...] = jnp.zeros(terms[last].shape, BF16)
     peaks[2 + last][...] = jnp.ones(peaks[2 + last].shape, F32)
+    peaks[4 + last][...] = jnp.ones(peaks[4 + last].shape, F32)
     score(start, 0, 0)
 
     @pl.loop(start, end)
@@ -69,7 +92,7 @@
                 blend(b, p - 1, 1 - slot)
             else:
                 blend(jnp.maximum(b - 1, start), pairs - 1, 1 - slot)
-            weigh(slot)
+            weigh(b, p, slot)
 
     blend(end - 1, pairs - 1, last)
 
@@ -122,6 +145,11 @@
     m1,
     m2,
     m3,
+    m4,
+    m5,
+    held_values,
+    held_totals,
+    held_peaks,
     send_sem,
     recv_sem,
     local_sem,
@@ -179,22 +207,23 @@
 
     edge_copies = to_face(0, 0, 1) + to_face(2, nb - 1, 1)
     step = nb // 2
-    near_copies = to_face(4, 1, step)
+    near_copies = to_face(4, 1, step // 2)
+    mid_copies = to_face(15, 1 + step // 2, step - step // 2)
     far_copies = to_face(13, 1 + step, nb - 2 - step)
     end_copies = [
         remote(6, tok4.at[0], ends.at[1], {"tile": up}),
         remote(7, tok4.at[nb - 1], ends.at[0], {"tile": down}),
     ]
     comp_copies = [
+        remote(9, wckv_hbm, wckv, {"comp": other}),
         remote(8, tok4, part, {"comp": other}),
-        remote(9, wckv_hbm, wckv, {"comp": other}),
         remote(10, gains_hbm, gains_p, {"comp": other}),
     ]
     corner_copies = [
         remote(11, side.at[1], side.at[nb + 1], {"tile": up}),
         remote(12, side.at[nb], side.at[0], {"tile": down}),
     ]
-    for copy in edge_copies + comp_copies + end_copies + near_copies + far_copies:
+    for copy in edge_copies + comp_copies + end_copies + near_copies + mid_copies + far_copies:
         copy.start()
     for copy in local[4:]:
         copy.start()
@@ -232,7 +261,7 @@
     def put_queries(ref, b, q):
         lane = lax.broadcasted_iota(jnp.int32, (1, d), 1)
         low = lax.rem(lane, pair) < pair // 2
-        q = q * float((d // HEADS) ** -0.5)
+        q = q * float((d // HEADS) ** -0.5 * LOG2E)
         q_low = jnp.where(low, q, 0.0).astype(BF16)
         q_high = jnp.where(low, 0.0, q).astype(BF16)
         for p in range(pairs):
@@ -263,10 +292,6 @@
             kwin[1 + base + j, pl.ds(0, cells)] = k[rows]
             put_values(vwin, 1 + base + j, pl.ds(0, cells), v[:, rows], jnp.full((1, cells), flags[j], F32))
 
-    for copy in edge_copies:
-        copy.wait_recv()
-    for copy in corner_copies:
-        copy.start()
     for copy in comp_copies:
         copy.wait_recv()
     wv_t[1] = wckv[:, d : 2 * d].T
@@ -285,57 +310,70 @@
             put_values(vcross, base + j, pl.ds(0, cells), v[:, rows], jnp.full((1, cells), flags[j], F32))
 
     def cross_keys(b, p):
-        return [kcross[links[comp, b, j], :, pl.ds(p * pair, pair)] for j in range(KC)]
+        return [kcross[links[comp, j, b], :, pl.ds(p * pair, pair)] for j in range(KC)]
 
     def cross_values(b, p):
-        return jnp.concatenate([vcross[links[comp, b, j], pl.ds(p * vrows, vrows)] for j in range(KC)], axis=1)
+        return jnp.concatenate([vcross[links[comp, j, b], pl.ds(p * vrows, vrows)] for j in range(KC)], axis=1)
 
     attend_bands(
-        0, nb, pairs, pair, cross_keys, cross_values, cqbd, cross_res,
-        (cs0, cs1), (ce0, ce1), (m0, m1, m2, m3),
+        0, nb, pairs, pair, cross_keys, cross_values, cqbd,
+        (cs0, cs1), (ce0, ce1), (m0, m1, m2, m3, m4, m5), result=cross_res,
     )
 
-    def window_kv(x, mask_col):
-        xa = (scaled(x) * gains[0:1, :].astype(F32) * mask_col).astype(BF16)
-        return dot(xa, wqkv[:, d : 2 * d]).astype(BF16), dot_t(wv_t[0], xa).astype(BF16)
-
     half = cells // 2
+    above, below = flag(tile > 0), flag(tile < n_tile - 1)
+
+    def window_kv(pieces):
+        flags, counts, rows = [], [], []
+        for ref, at, row_flags in pieces:
+            rows.append(ref[at].astype(F32).reshape(cells, d))
+            flags += row_flags
+            counts += [cells // len(row_flags)] * len(row_flags)
+        x = scaled(jnp.concatenate(rows, axis=0))
+        xa = (x * gains[0:1, :].astype(F32) * expand(flags, counts, 0)).astype(BF16)
+        k, v = dot(xa, wqkv[:, d : 2 * d]).astype(BF16), dot_t(wv_t[0], xa).astype(BF16)
+        return k, v
+
+    def put_window(pieces, places, lane):
+        k, v = window_kv(pieces)
+        for j, ((_, _, row_flags), at) in enumerate(zip(pieces, places)):
+            rows = slice(j * cells, (j + 1) * cells)
+            kwin[at, pl.ds(lane, cells)] = k[rows]
+            row = expand(row_flags, [cells // len(row_flags)] * len(row_flags), 1)
+            put_values(vwin, at, pl.ds(lane, cells), v[:, rows], row)
 
     def beside(bands):
-        flags = []
-        for at in bands:
-            flags += [usable(tile, left, at), usable(tile, right, at)]
-        x = jnp.concatenate([side[1 + at].astype(F32).reshape(cells, d) for at in bands], axis=0)
-        k, v = window_kv(x, expand(flags, [half] * len(flags), 0))
-        for j, at in enumerate(bands):
-            rows = slice(j * cells, (j + 1) * cells)
-            kwin[1 + at, pl.ds(cells, cells)] = k[rows]
-            put_values(
-                vwin, 1 + at, pl.ds(cells, cells), v[:, rows], expand(flags[2 * j : 2 * j + 2], [half] * 2, 1)
-            )
-
-    for copy in end_copies + corner_copies:
+        return [(side, 1 + at, [usable(tile, left, at), usable(tile, right, at)]) for at in bands]
+
+    for copy in edge_copies:
         copy.wait_recv()
-    above, below = flag(tile > 0), flag(tile < n_tile - 1)
-    flags, counts = [], [cells, half, half]
-    for inside, row, band in ((above, up, nb - 1), (below, down, 0)):
-        flags.append([inside * usable(row, at, band) for at in (face, left, right)])
-    rim = jnp.concatenate(
-        [ref[at].astype(F32).reshape(cells, d) for ref, at in ((ends, 0), (side, 0), (ends, 1), (side, nb + 1))],
-        axis=0,
+    for copy in corner_copies:
+        copy.start()
+    for copy in end_copies:
+        copy.wait_recv()
+    put_window(
+        [(ends, 0, [above * usable(up, face, nb - 1)]), (ends, 1, [below * usable(down, face, 0)])], (0, nb + 1), 0
     )
-    k, v = window_kv(rim, expand(flags[0] + flags[1], counts + counts, 0))
-    for j, at in enumerate((0, nb + 1)):
-        rows = slice(j * 2 * cells, (j + 1) * 2 * cells)
-        kwin[at] = k[rows]
-        put_values(vwin, at, pl.ds(0, 2 * cells), v[:, rows], expand(flags[j], counts, 1))
-    beside((0, nb - 1))
-
-    def window_keys(b, p):
-        return [kwin[b + j, :, pl.ds(p * pair, pair)] for j in range(3)]
-
-    def window_values(b, p):
-        return jnp.concatenate([vwin[b + j, pl.ds(p * vrows, vrows)] for j in range(3)], axis=1)
+
+    def window_keys(lane):
+        return lambda b, p: [kwin[b + j, pl.ds(lane, cells), pl.ds(p * pair, pair)] for j in range(3)]
+
+    def window_values(lane):
+        return lambda b, p: jnp.concatenate(
+            [vwin[b + j, pl.ds(p * vrows, vrows), pl.ds(lane, cells)] for j in range(3)], axis=1
+        )
+
+    held = (held_values, held_totals, held_peaks)
+    attend_bands(
+        0, nb, pairs, pair, window_keys(0), window_values(0), qbd,
+        (ws0, ws1), (we0, we1), (m0, m1, m2, m3, m4, m5), held=held,
+    )
+
+    def attend_sides(start, end):
+        attend_bands(
+            start, end, pairs, pair, window_keys(cells), window_values(cells), qbd,
+            (ws0, ws1), (we0, we1), (m0, m1, m2, m3, m4, m5), result=win_res, held=held,
+        )
 
     ff = wup.shape[1]
     part_ff = ff // 4
@@ -354,23 +392,33 @@
             total = piece if total is None else total + piece
         out_ref[pl.ds(base * cells, chunk), :] = (middle + live * total).astype(BF16)
 
-    for base, copies, bands in (
-        (0, near_copies, range(1, 1 + step)),
-        (step, far_copies, range(1 + step, nb - 1)),
-    ):
-        for copy in copies:
-            copy.wait_recv()
-        beside(bands)
-        attend_bands(
-            base, base + step, pairs, pair, window_keys, window_values, qbd, win_res,
-            (ws0, ws1), (we0, we1), (m0, m1, m2, m3),
-        )
-        if base == 0:
-            for copy in local[4:]:
-                copy.wait()
-        finish(base)
-
-    for copy in edge_copies + near_copies + far_copies + end_copies + comp_copies + corner_copies:
+    for copy in corner_copies + near_copies:
+        copy.wait_recv()
+    corners = [
+        (side, 0, [above * usable(up, at, nb - 1) for at in (left, right)]),
+        (side, nb + 1, [below * usable(down, at, 0) for at in (left, right)]),
+    ]
+    bands = [0, nb - 1] + list(range(1, 1 + step // 2))
+    put_window(corners + beside(bands), [0, nb + 1] + [1 + at for at in bands], cells)
+    attend_sides(0, step // 2)
+
+    for copy in mid_copies:
+        copy.wait_recv()
+    bands = list(range(1 + step // 2, 1 + step))
+    put_window(beside(bands), [1 + at for at in bands], cells)
+    attend_sides(step // 2, step)
+    for copy in local[4:]:
+        copy.wait()
+    finish(0)
+
+    for copy in far_copies:
+        copy.wait_recv()
+    bands = list(range(1 + step, nb - 1))
+    put_window(beside(bands), [1 + at for at in bands], cells)
+    attend_sides(step, nb)
+    finish(step)
+
+    for copy in edge_copies + near_copies + mid_copies + far_copies + end_copies + comp_copies + corner_copies:
         copy.wait_send()
 
 
@@ -394,7 +442,7 @@
     ff = up_weight.shape[2]
     pair = 2 * (d // HEADS)
     vrows = (d // pair) * (pair + EXTRA)
-    links = intersection_list.reshape(2, nb, KC)
+    links = jnp.transpose(intersection_list, (0, 2, 3, 1)).reshape(2, KC, nb)
     smem = pl.BlockSpec(memory_space=pltpu.SMEM)
     hbm = pl.BlockSpec(memory_space=pl.ANY)
     out = pl.pallas_call(
@@ -427,11 +475,14 @@
             pltpu.VMEM((nb, cells, d), BF16),
             *[pltpu.VMEM((KC * cells, 2 * cells), F32)] * 2,
             *[pltpu.VMEM((KC * cells, 2 * cells), BF16)] * 2,
-            *[pltpu.VMEM((6 * cells, 2 * cells), F32)] * 2,
-            *[pltpu.VMEM((6 * cells, 2 * cells), BF16)] * 2,
-            *[pltpu.VMEM((8, 2 * cells), F32)] * 4,
-            pltpu.SemaphoreType.DMA((15,)),
-            pltpu.SemaphoreType.DMA((15,)),
+            *[pltpu.VMEM((3 * cells, 2 * cells), F32)] * 2,
+            *[pltpu.VMEM((3 * cells, 2 * cells), BF16)] * 2,
+            *[pltpu.VMEM((8, 2 * cells), F32)] * 6,
+            pltpu.VMEM((nb, d // pair, pair // 2, 2 * cells), F32),
+            pltpu.VMEM((nb, d // pair, 8, 2 * cells), F32),
+            pltpu.VMEM((nb, d // pair, 8, 2 * cells), F32),
+            pltpu.SemaphoreType.DMA((17,)),
+            pltpu.SemaphoreType.DMA((17,)),
             pltpu.SemaphoreType.DMA((8,)),
         ],
         compiler_params=pltpu.CompilerParams(

time: 50 us -> 46 us (0.920)
  Pallas kernels: 46 us -> 43.6 us
  local copies, waits for them, and re-layouts: 3.63 us -> 2.26 us
    pallas_call x1, Pallas kernels: 46 us -> 43.6 us  [per_device(): pl.pallas_call(kernel, out_shape=jax.ShapeDtypeStruct((nb * cells, d), BF...]
    reshape x1 -> x0, local copies, waits for them, and re-layouts: 1.36 us -> none  [per_device(): links = intersection_list.reshape(2, nb, KC)]
where the time goes in v1:
time: 46 us; the launch traced here: 45.8 us
  Pallas kernels  43.6 us (95%)
  local copies, waits for them, and re-layouts  2.26 us (5%)
    pallas_call x1, Pallas kernels, per_device(): pl.pallas_call(kernel, out_shape=jax.ShapeDtypeStruct((nb * cells, d), BF...  43.6 us
    unnamed x1, local copies, waits for them, and re-layouts  2.26 us

profile of v1, /device:TPU:0, one launch (start us, length us, event | category | flops | bytes accessed | tf_op | source)
XLA Modules:
  0.0 45.8 jit_solution(9891961828185653546)
XLA Ops:
  0.0 43.6 %shard_map.109 = bf16[1024,512]{1,0:T(8,128)(2,1)} custom-call(s32[2,4,8]{2,1,0:T(4,128)} %bitcast.24, s32[4,4]{1,0:T(4,128)} %land.1, bf16[8,8,2,8,512]{4,3,2,1,0:T(8,128)(2,1)} %bitcast.15, bf16[8,16,8,512]{3,2,1,0:T(8,128)(2,1)} %bitcast.16, bf16[3,512]{1,0:T(4,128)(2,1)} %bitcast.25, bf16[512,1536]{1,0:T(8,128)(2,1)} %bitcast.19, ...), custom_call_target="tpu_custom_call" | custom-call | tf_op jit(solution)/shard_map/pallas_call | solution.py:448
  43.6 2.3 %copy.13 = bf16[1,64,16,512]{3,2,1,0:T(8,128)(2,1)} copy(bf16[1,64,16,512]{3,2,1,0:T(8,128)(2,1)} %bitcast.14) | data formatting | bytes 2097152

commit v2 on v1

--- a/solution.py
+++ b/solution.py
@@ -26,11 +26,12 @@
     return lax.dot_general(a, b, (((1,), (1,)), ((), ())), preferred_element_type=F32)
 
 
-def attend_bands(start, end, pairs, pair, keys_of, values_of, queries, scores, terms, peaks, result=None, held=None):
+def attend_bands(start, end, pairs, pair, keys_of, values_of, queries, scores, terms, peaks, result=None, held=None, stride=1, hook=None):
     cells = queries.shape[2] // 2
     half = pair // 2
 
-    def score(b, p, slot):
+    def score(i, p, slot):
+        b = i * stride
         q = queries[b, p]
         top = jnp.zeros((8, 2 * cells), F32)
         if result is not None and held is not None:
@@ -44,7 +45,8 @@
             row += rows
         peaks[slot][...] = jnp.broadcast_to(jnp.max(top, axis=0, keepdims=True), (8, 2 * cells))
 
-    def blend(b, p, slot):
+    def blend(i, p, slot):
+        b = i * stride
         blended = dot(values_of(b, p), terms[slot][...])
         first, second = blended[:half, :cells], blended[half:pair, cells:]
         total = blended[pair : pair + 8, :]
@@ -64,7 +66,8 @@
         second = second * inverse[:, cells:]
         result[b, :, pl.ds(p * pair, pair)] = jnp.concatenate([first, second], axis=0).T.astype(BF16)
 
-    def weigh(b, p, slot):
+    def weigh(i, p, slot):
+        b = i * stride
         peak = peaks[slot][0:1, :]
         terms[slot][...] = jnp.exp2(scores[slot][...] - peak).astype(BF16)
         if result is None:
@@ -82,6 +85,8 @@
 
     @pl.loop(start, end)
     def _(b):
+        if hook is not None:
+            hook(b)
         for p in range(pairs):
             slot = p % 2
             if p + 1 < pairs:
@@ -141,6 +146,7 @@
     ws1,
     we0,
     we1,
+    out_all,
     m0,
     m1,
     m2,
@@ -153,6 +159,7 @@
     send_sem,
     recv_sem,
     local_sem,
+    out_sem,
 ):
     nb, groups, _, d = own.shape
     cells = groups * BR
@@ -186,7 +193,6 @@
     barrier = pltpu.get_barrier_semaphore()
     for target in ({"comp": other}, {"face": left}, {"face": right}, {"tile": up}, {"tile": down}):
         pl.semaphore_signal(barrier, inc=1, device_id=target, device_id_type=MESH)
-    pl.semaphore_wait(barrier, 5)
 
     def remote(i, src, dst, target):
         return pltpu.make_async_remote_copy(
@@ -216,17 +222,36 @@
     ]
     comp_copies = [
         remote(9, wckv_hbm, wckv, {"comp": other}),
-        remote(8, tok4, part, {"comp": other}),
         remote(10, gains_hbm, gains_p, {"comp": other}),
     ]
+
+    def part_copy(c):
+        bands = pl.ds(c * step, step)
+        return remote(17 + c, tok4.at[bands], part.at[bands], {"comp": other})
+
+    part_copies = [part_copy(c) for c in range(nb // step)]
     corner_copies = [
         remote(11, side.at[1], side.at[nb + 1], {"tile": up}),
         remote(12, side.at[nb], side.at[0], {"tile": down}),
     ]
-    for copy in edge_copies + comp_copies + end_copies + near_copies + mid_copies + far_copies:
-        copy.start()
-    for copy in local[4:]:
-        copy.start()
+
+    has_up, has_down = tile > 0, tile < n_tile - 1
+
+    def along_tile(copies, action):
+        upward, downward = copies
+        first, second = (has_down, has_up) if action == "wait_recv" else (has_up, has_down)
+        pl.when(first)(getattr(upward, action))
+        pl.when(second)(getattr(downward, action))
+
+    @pl.when(jnp.logical_not(has_up))
+    def _():
+        ends[0] = jnp.zeros(ends.shape[1:], BF16)
+        side[0] = jnp.zeros(side.shape[1:], BF16)
+
+    @pl.when(jnp.logical_not(has_down))
+    def _():
+        ends[1] = jnp.zeros(ends.shape[1:], BF16)
+        side[nb + 1] = jnp.zeros(side.shape[1:], BF16)
 
     is_air = comp == 0
     own_land = land[tile, face]
@@ -275,6 +300,17 @@
 
     @pl.loop(0, nb // step)
     def _(c):
+        @pl.when(c == nb // step - 1)
+        def _():
+            pl.semaphore_wait(barrier, 5)
+            for copy in comp_copies + part_copies[:1] + edge_copies + part_copies[1:]:
+                copy.start()
+            along_tile(end_copies, "start")
+            for copy in near_copies:
+                copy.start()
+            for copy in local[4:]:
+                copy.start()
+
         base = c * step
         x = own[pl.ds(base, step)].astype(F32).reshape(chunk, d)
         x = scaled(x)
@@ -292,6 +328,21 @@
             kwin[1 + base + j, pl.ds(0, cells)] = k[rows]
             put_values(vwin, 1 + base + j, pl.ds(0, cells), v[:, rows], jnp.full((1, cells), flags[j], F32))
 
+
+    def window_keys(lane):
+        return lambda b, p: [kwin[b + j, pl.ds(lane, cells), pl.ds(p * pair, pair)] for j in range(3)]
+
+    def window_values(lane):
+        return lambda b, p: jnp.concatenate(
+            [vwin[b + j, pl.ds(p * vrows, vrows), pl.ds(lane, cells)] for j in range(3)], axis=1
+        )
+
+    held = (held_values, held_totals, held_peaks)
+    attend_bands(
+        1, nb - 1, pairs, pair, window_keys(0), window_values(0), qbd,
+        (ws0, ws1), (we0, we1), (m0, m1, m2, m3, m4, m5), held=held,
+    )
+
     for copy in comp_copies:
         copy.wait_recv()
     wv_t[1] = wckv[:, d : 2 * d].T
@@ -299,6 +350,7 @@
     @pl.loop(0, nb // step)
     def _(c):
         base = c * step
+        part_copy(c).wait_recv()
         x = scaled(part[pl.ds(base, step)].astype(F32).reshape(chunk, d))
         flags = [flag((comp == 1) | (base + j >= own_land)) for j in range(step)]
         xp = (x * gains_p[1:2, :].astype(F32) * expand(flags, [cells] * step, 0)).astype(BF16)
@@ -315,9 +367,18 @@
     def cross_values(b, p):
         return jnp.concatenate([vcross[links[comp, j, b], pl.ds(p * vrows, vrows)] for j in range(KC)], axis=1)
 
+    def relay(b):
+        @pl.when(b == nb // 2)
+        def _():
+            for copy in edge_copies:
+                copy.wait_recv()
+            along_tile(corner_copies, "start")
+            for copy in mid_copies + far_copies:
+                copy.start()
+
     attend_bands(
         0, nb, pairs, pair, cross_keys, cross_values, cqbd,
-        (cs0, cs1), (ce0, ce1), (m0, m1, m2, m3, m4, m5), result=cross_res,
+        (cs0, cs1), (ce0, ce1), (m0, m1, m2, m3, m4, m5), result=cross_res, hook=relay,
     )
 
     half = cells // 2
@@ -345,28 +406,14 @@
     def beside(bands):
         return [(side, 1 + at, [usable(tile, left, at), usable(tile, right, at)]) for at in bands]
 
-    for copy in edge_copies:
-        copy.wait_recv()
-    for copy in corner_copies:
-        copy.start()
-    for copy in end_copies:
-        copy.wait_recv()
+    along_tile(end_copies, "wait_recv")
     put_window(
         [(ends, 0, [above * usable(up, face, nb - 1)]), (ends, 1, [below * usable(down, face, 0)])], (0, nb + 1), 0
     )
 
-    def window_keys(lane):
-        return lambda b, p: [kwin[b + j, pl.ds(lane, cells), pl.ds(p * pair, pair)] for j in range(3)]
-
-    def window_values(lane):
-        return lambda b, p: jnp.concatenate(
-            [vwin[b + j, pl.ds(p * vrows, vrows), pl.ds(lane, cells)] for j in range(3)], axis=1
-        )
-
-    held = (held_values, held_totals, held_peaks)
     attend_bands(
-        0, nb, pairs, pair, window_keys(0), window_values(0), qbd,
-        (ws0, ws1), (we0, we1), (m0, m1, m2, m3, m4, m5), held=held,
+        0, 2, pairs, pair, window_keys(0), window_values(0), qbd,
+        (ws0, ws1), (we0, we1), (m0, m1, m2, m3, m4, m5), held=held, stride=nb - 1,
     )
 
     def attend_sides(start, end):
@@ -377,6 +424,11 @@
 
     ff = wup.shape[1]
     part_ff = ff // 4
+
+    def out_copy(base, j):
+        at = pl.ds(base * cells + j * (chunk // 2), chunk // 2)
+        i = 2 * (base // step) + j
+        return pltpu.make_async_copy(out_all.at[at], out_ref.at[at], out_sem.at[i])
 
     def finish(base):
         live = expand([flag(is_air | (base + j >= own_land)) for j in range(step)], [cells] * step, 0)
@@ -385,14 +437,22 @@
         middle = own[pl.ds(base, step)].astype(F32).reshape(chunk, d) + live * update
         mlp_input = (scaled(middle) * gains[2:3, :].astype(F32)).astype(BF16)
         total = None
-        for f in range(4):
+        for f in range(3):
             cols = slice(f * part_ff, (f + 1) * part_ff)
             hidden = jax.nn.silu(dot(mlp_input, wup[:, cols])).astype(BF16)
             piece = dot(hidden, wdown[cols, :])
             total = piece if total is None else total + piece
-        out_ref[pl.ds(base * cells, chunk), :] = (middle + live * total).astype(BF16)
-
-    for copy in corner_copies + near_copies:
+        cols = slice(3 * part_ff, ff)
+        hidden = jax.nn.silu(dot(mlp_input, wup[:, cols])).astype(BF16)
+        for j in range(2):
+            rows = slice(j * chunk // 2, (j + 1) * chunk // 2)
+            piece = total[rows] + dot(hidden[rows], wdown[cols, :])
+            at = pl.ds(base * cells + j * (chunk // 2), chunk // 2)
+            out_all[at, :] = (middle[rows] + live[rows] * piece).astype(BF16)
+            out_copy(base, j).start()
+
+    along_tile(corner_copies, "wait_recv")
+    for copy in near_copies:
         copy.wait_recv()
     corners = [
         (side, 0, [above * usable(up, at, nb - 1) for at in (left, right)]),
@@ -418,8 +478,13 @@
     attend_sides(step, nb)
     finish(step)
 
-    for copy in edge_copies + near_copies + mid_copies + far_copies + end_copies + comp_copies + corner_copies:
+    for copy in edge_copies + near_copies + mid_copies + far_copies + comp_copies + part_copies:
         copy.wait_send()
+    along_tile(end_copies, "wait_send")
+    along_tile(corner_copies, "wait_send")
+    for base in range(0, nb, step):
+        for j in range(2):
+            out_copy(base, j).wait()
 
 
 def per_device(
@@ -449,7 +514,7 @@
         kernel,
         out_shape=jax.ShapeDtypeStruct((nb * cells, d), BF16),
         in_specs=[smem] * 2 + [hbm] * 10,
-        out_specs=pl.BlockSpec(memory_space=pltpu.VMEM),
+        out_specs=hbm,
         scratch_shapes=[
             pltpu.VMEM((nb, groups, BR, d), BF16),
             pltpu.VMEM((nb + 2, groups, BR, d), BF16),
@@ -477,13 +542,15 @@
             *[pltpu.VMEM((KC * cells, 2 * cells), BF16)] * 2,
             *[pltpu.VMEM((3 * cells, 2 * cells), F32)] * 2,
             *[pltpu.VMEM((3 * cells, 2 * cells), BF16)] * 2,
+            pltpu.VMEM((nb * cells, d), BF16),
             *[pltpu.VMEM((8, 2 * cells), F32)] * 6,
             pltpu.VMEM((nb, d // pair, pair // 2, 2 * cells), F32),
             pltpu.VMEM((nb, d // pair, 8, 2 * cells), F32),
             pltpu.VMEM((nb, d // pair, 8, 2 * cells), F32),
-            pltpu.SemaphoreType.DMA((17,)),
-            pltpu.SemaphoreType.DMA((17,)),
+            pltpu.SemaphoreType.DMA((19,)),
+            pltpu.SemaphoreType.DMA((19,)),
             pltpu.SemaphoreType.DMA((8,)),
+            pltpu.SemaphoreType.DMA((2 * nb // (nb // 2),)),
         ],
         compiler_params=pltpu.CompilerParams(
             collective_id=0, has_side_effects=True, vmem_limit_bytes=56 * 1024 * 1024

time: 46 us -> 42 us (0.913)
  Pallas kernels: 43.6 us -> 39.5 us
    pallas_call x1, Pallas kernels: 43.6 us -> 39.5 us  [per_device(): pl.pallas_call(kernel, out_shape=jax.ShapeDtypeStruct((nb * cells, d), BF...]
where the time goes in v2:
time: 42 us; the launch traced here: 41.8 us
  Pallas kernels  39.5 us (94%)
  local copies, waits for them, and re-layouts  2.26 us (5%)
    pallas_call x1, Pallas kernels, per_device(): pl.pallas_call(kernel, out_shape=jax.ShapeDtypeStruct((nb * cells, d), BF...  39.5 us
    unnamed x1, local copies, waits for them, and re-layouts  2.26 us

profile of v2, /device:TPU:0, one launch (start us, length us, event | category | flops | bytes accessed | tf_op | source)
XLA Modules:
  0.0 41.8 jit_solution(6306727253309889930)
XLA Ops:
  0.0 39.5 %shard_map.109 = bf16[1024,512]{1,0:T(8,128)(2,1)} custom-call(s32[2,4,8]{2,1,0:T(4,128)} %bitcast.24, s32[4,4]{1,0:T(4,128)} %land.1, bf16[8,8,2,8,512]{4,3,2,1,0:T(8,128)(2,1)} %bitcast.15, bf16[8,16,8,512]{3,2,1,0:T(8,128)(2,1)} %bitcast.16, bf16[3,512]{1,0:T(4,128)(2,1)} %bitcast.25, bf16[512,1536]{1,0:T(8,128)(2,1)} %bitcast.19, ...), custom_call_target="tpu_custom_call" | custom-call | tf_op jit(solution)/shard_map/pallas_call | solution.py:513
  39.5 2.3 %copy.13 = bf16[1,64,16,512]{3,2,1,0:T(8,128)(2,1)} copy(bf16[1,64,16,512]{3,2,1,0:T(8,128)(2,1)} %bitcast.14) | data formatting | bytes 2097152
